TPU v7x, 512 devices: a whole 4x4x16 slice. The times are simulated.
512 devices in a mesh: mem: 32 (over z, core), space: 16 (over y, x).
Axes of the slice: x: 4, y: 4, z: 16, core: 2. Of those that a mesh axis runs over, the one named last changes fastest.
Arguments:
- ensemble: bfloat16 [1024, 262144], P('mem', 'space'), may hold values from -420 to 420, as said below
- log_weights: float32 [1024], replicated, may hold values from -405 to -195, as said below
Outputs:
- analysis: bfloat16 [1024, 262144], P('mem', 'space')
Inputs may be any that keep to these rules, and one draw needn't show every extreme that they name: `ensemble`: finite values. `log_weights`: unnormalized log-likelihoods; only differences between members matter.
All inputs are finite; a program needn't handle non-finite values.
Results may differ from a plain program's by a relative error of at most 0.003.
The roundings to bfloat16 on the way count: a program that leaves them out, or rounds other values in their place, can miss the bound.
Values may be sent and summed in bfloat16 or wider, within the bound.
No kernel may reach another device: no remote copies, remote signals or barrier semaphores. Data moves between devices by JAX's collectives and lax.ppermute only.
A program may use at most 64 MiB of HBM per device.

v0:
```python
import jax
import jax.numpy as jnp
from jax import lax
from jax.sharding import PartitionSpec as P

M = 1024
ITERS = 10


def coupling_from(kernel_part, weights_part, total_sum):

    def sweep(step, carry):
        row_scale, col_scale = carry
        row_scale = weights_part / jnp.dot(kernel_part, col_scale, precision=lax.Precision.HIGHEST)
        sums = total_sum(jnp.dot(row_scale, kernel_part, precision=lax.Precision.HIGHEST))
        return (row_scale, 1.0 / M / sums)

    start_col = jnp.ones((kernel_part.shape[1],), jnp.float32)
    row_scale, col_scale = lax.fori_loop(0, ITERS, sweep, (weights_part, start_col))
    return (M * row_scale[:, None] * kernel_part * col_scale[None, :]).astype(jnp.bfloat16)


def per_device(ensemble, log_weights):
    members_dev = ensemble.shape[0]
    cells_total = ensemble.shape[1] * lax.axis_size("space")
    relaid = lax.all_to_all(ensemble, "mem", split_axis=1, concat_axis=0, tiled=True)
    partial_gram = lax.dot_general(
        relaid, relaid, (((1,), (1,)), ((), ())), preferred_element_type=jnp.float32
    )
    weights = jax.nn.softmax(log_weights)
    local_rows = lax.psum_scatter(partial_gram, "mem", scatter_dimension=0, tiled=True)
    gram_rows = lax.psum(local_rows, "space")
    start = lax.axis_index("mem") * members_dev
    own_block = lax.dynamic_slice_in_dim(gram_rows, start, members_dev, 1)
    own_norms = jnp.sum(own_block * jnp.eye(members_dev, dtype=jnp.float32), axis=1)
    all_norms = lax.all_gather(own_norms, "mem", axis=0, tiled=True)
    dist = (own_norms[:, None] + all_norms[None, :] - 2.0 * gram_rows) / cells_total
    dist_total = lax.psum(jnp.sum(dist), "mem")
    mean_dist = dist_total / (M * (M - 1))
    kernel = jnp.exp(-dist / (0.08 * mean_dist))
    weights_rows = lax.dynamic_slice_in_dim(weights, start, members_dev, 0)

    def column_total(values):
        return lax.psum(values, "mem")

    coupling_rows = coupling_from(kernel, weights_rows, column_total)
    coupling = lax.all_gather(coupling_rows, "mem", axis=0, tiled=True)
    mixed = lax.dot_general(
        coupling, relaid, (((0,), (0,)), ((), ())), preferred_element_type=jnp.float32
    )
    mixed = mixed.astype(jnp.bfloat16)
    return lax.all_to_all(mixed, "mem", split_axis=0, concat_axis=1, tiled=True)


def solution(mesh):
    return jax.shard_map(
        per_device,
        mesh=mesh,
        in_specs=(P("mem", "space"), P()),
        out_specs=P("mem", "space"),
        check_vma=False,
    )
```

profile of v0, /device:TPU:1, one launch (start us, length us, event | category | flops | bytes accessed | tf_op | source)
XLA Modules:
  0.0 1010.4 jit_solution(11346003454657286297)
XLA Ops:
  6.5 1.4 copy.12
  7.9 72.3 %all_to_all.38 = bf16[32,32,512]{2,0,1:T(8,128)(2,1)S(1)} all-to-all(bf16[32,32,512]{2,0,1:T(8,128)(2,1)S(1)} %bitcast.43), channel_id=1, replica_groups=mesh['mem'=32,'space'=16] {'mem'}, dimensions={1} | all-to-all | bytes 2097152 | tf_op jit(solution)/shard_map/all_to_all | solution.py:26
  80.2 3.2 fusion.6
  83.5 1.3 dynamic-slice
  85.3 0.6 reduce_max.9
  85.9 1.2 fusion.5
  87.2 98.8 %reduce-scatter.2.cloned.1.call-done = f32[32,1024]{1,0:T(8,128)} async-done(((f32[1024,1024]{1,0:T(8,128)}), f32[32,1024]{1,0:T(8,128)}) %reduce-scatter.2.cloned.1.call-update) | async-done | bytes 131088 | tf_op jit(solution)/shard_map/reduce_scatter | solution.py:31
  186.1 1.2 fusion.4
  187.4 114.0 %all-reduce.3.cloned.1.call-done = f32[32,1024]{1,0:T(8,128)} async-done(((f32[32,1024]{1,0:T(8,128)}), f32[32,1024]{1,0:T(8,128)}) %all-reduce.3.cloned.1.call-update) | async-done | bytes 131088 | tf_op jit(solution)/shard_map/psum | solution.py:32
  301.4 1.0 select_reduce_fusion
  302.7 48.6 %all-reduce = f32[1024]{0:T(1024)S(1)} all-reduce(f32[1024]{0:T(1024)S(1)} %dynamic-update-slice), channel_id=1, replica_groups=mesh['mem'=32,'space'=16] {'mem'}, use_global_device_ids=true, to_apply=%add | all-reduce | flops 1024 | bytes 8192
  351.2 1.7 fusion.3
  352.9 0.5 copy.16
  353.4 47.1 %psum.22 = f32[]{:T(128)} all-reduce(f32[]{:T(128)} %fusion.3), channel_id=1, replica_groups=mesh['mem'=32,'space'=16] {'mem'}, use_global_device_ids=true, to_apply=%region_6.0 | all-reduce | flops 1 | bytes 8 | tf_op jit(solution)/shard_map/psum | solution.py:38
  401.2 1.0 divide_exponential_fusion
  402.2 462.6 %while.13 = (s32[]{:T(128)}, f32[32]{0:T(128)}, f32[1024]{0:T(1024)S(1)}, f32[32,1024]{1,0:T(8,128)S(1)}, f32[32]{0:T(128)S(1)}, /*index=5*/s32[]{:T(128)}, s32[]{:T(128)}) while((s32[]{:T(128)}, f32[32]{0:T(128)}, f32[1024]{0:T(1024)S(1)}, f32[32,1024]{1,0:T(8,128)S(1)}, f32[32]{0:T(128)S(1)}, /*index=5*/s32[]{:T(128)}, ...), condition=%wide.region_9.0_spmd.clone, body=%wide.region_7.0_spmd.clone.sunk | while | flops 789539 | bytes 295923 | solution.py:19
  402.6 45.8 %psum.25 = f32[1024]{0:T(1024)S(1)} all-reduce(f32[1024]{0:T(1024)S(1)} %bitcast.49), channel_id=1, replica_groups=mesh['mem'=32,'space'=16] {'mem'}, use_global_device_ids=true, to_apply=%region_8.0 | all-reduce | flops 1024 | bytes 8192 | tf_op jit(solution)/shard_map/while/body/eval_jaxpr/psum | solution.py:44
  448.9 45.8 %psum.25 = f32[1024]{0:T(1024)S(1)} all-reduce(f32[1024]{0:T(1024)S(1)} %bitcast.49), channel_id=1, replica_groups=mesh['mem'=32,'space'=16] {'mem'}, use_global_device_ids=true, to_apply=%region_8.0 | all-reduce | flops 1024 | bytes 8192 | tf_op jit(solution)/shard_map/while/body/eval_jaxpr/psum | solution.py:44
  495.2 45.8 %psum.25 = f32[1024]{0:T(1024)S(1)} all-reduce(f32[1024]{0:T(1024)S(1)} %bitcast.49), channel_id=1, replica_groups=mesh['mem'=32,'space'=16] {'mem'}, use_global_device_ids=true, to_apply=%region_8.0 | all-reduce | flops 1024 | bytes 8192 | tf_op jit(solution)/shard_map/while/body/eval_jaxpr/psum | solution.py:44
  541.4 45.8 %psum.25 = f32[1024]{0:T(1024)S(1)} all-reduce(f32[1024]{0:T(1024)S(1)} %bitcast.49), channel_id=1, replica_groups=mesh['mem'=32,'space'=16] {'mem'}, use_global_device_ids=true, to_apply=%region_8.0 | all-reduce | flops 1024 | bytes 8192 | tf_op jit(solution)/shard_map/while/body/eval_jaxpr/psum | solution.py:44
  587.7 45.8 %psum.25 = f32[1024]{0:T(1024)S(1)} all-reduce(f32[1024]{0:T(1024)S(1)} %bitcast.49), channel_id=1, replica_groups=mesh['mem'=32,'space'=16] {'mem'}, use_global_device_ids=true, to_apply=%region_8.0 | all-reduce | flops 1024 | bytes 8192 | tf_op jit(solution)/shard_map/while/body/eval_jaxpr/psum | solution.py:44
  633.9 45.8 %psum.25 = f32[1024]{0:T(1024)S(1)} all-reduce(f32[1024]{0:T(1024)S(1)} %bitcast.49), channel_id=1, replica_groups=mesh['mem'=32,'space'=16] {'mem'}, use_global_device_ids=true, to_apply=%region_8.0 | all-reduce | flops 1024 | bytes 8192 | tf_op jit(solution)/shard_map/while/body/eval_jaxpr/psum | solution.py:44
  680.2 45.8 %psum.25 = f32[1024]{0:T(1024)S(1)} all-reduce(f32[1024]{0:T(1024)S(1)} %bitcast.49), channel_id=1, replica_groups=mesh['mem'=32,'space'=16] {'mem'}, use_global_device_ids=true, to_apply=%region_8.0 | all-reduce | flops 1024 | bytes 8192 | tf_op jit(solution)/shard_map/while/body/eval_jaxpr/psum | solution.py:44
  726.5 45.8 %psum.25 = f32[1024]{0:T(1024)S(1)} all-reduce(f32[1024]{0:T(1024)S(1)} %bitcast.49), channel_id=1, replica_groups=mesh['mem'=32,'space'=16] {'mem'}, use_global_device_ids=true, to_apply=%region_8.0 | all-reduce | flops 1024 | bytes 8192 | tf_op jit(solution)/shard_map/while/body/eval_jaxpr/psum | solution.py:44
  772.7 45.8 %psum.25 = f32[1024]{0:T(1024)S(1)} all-reduce(f32[1024]{0:T(1024)S(1)} %bitcast.49), channel_id=1, replica_groups=mesh['mem'=32,'space'=16] {'mem'}, use_global_device_ids=true, to_apply=%region_8.0 | all-reduce | flops 1024 | bytes 8192 | tf_op jit(solution)/shard_map/while/body/eval_jaxpr/psum | solution.py:44
  819.0 45.8 %psum.25 = f32[1024]{0:T(1024)S(1)} all-reduce(f32[1024]{0:T(1024)S(1)} %bitcast.49), channel_id=1, replica_groups=mesh['mem'=32,'space'=16] {'mem'}, use_global_device_ids=true, to_apply=%region_8.0 | all-reduce | flops 1024 | bytes 8192 | tf_op jit(solution)/shard_map/while/body/eval_jaxpr/psum | solution.py:44
  864.8 0.6 broadcast_multiply_fusion
  865.4 0.7 multiply_convert_fusion
  866.2 70.0 %all-gather.2.cloned.1.call-done = bf16[1024,1024]{1,0:T(8,128)(2,1)} async-done(((bf16[32,1024]{1,0:T(8,128)(2,1)}), bf16[1024,1024]{1,0:T(8,128)(2,1)}) %all-gather.2.cloned.1.call-update) | async-done | bytes 2097168 | tf_op jit(solution)/shard_map/all_gather | solution.py:47
  936.2 2.9 convolution_convert_fusion
  939.0 63.8 %all_to_all.39 = bf16[32,32,512]{2,1,0:T(8,128)(2,1)S(1)} all-to-all(bf16[32,32,512]{2,1,0:T(8,128)(2,1)S(1)} %bitcast.47), channel_id=1, replica_groups=mesh['mem'=32,'space'=16] {'mem'}, dimensions={0} | all-to-all | bytes 2097152 | tf_op jit(solution)/shard_map/all_to_all | solution.py:52
  1002.8 1.1 copy.10
  (74 shorter events, 4.7 us)
Async XLA Ops:
  6.5 179.5 %reduce-scatter.2.cloned.1.call-start = ((), (), s32[]{:S(2)}) async-start(), calls=%async_computation.3 | async-start | bytes 4325376 | tf_op jit(solution)/shard_map/reduce_scatter | solution.py:31
  83.4 1.9 copy-start.1
  83.4 218.0 %all-reduce.3.cloned.1.call-start = ((), (), s32[]{:S(2)}) async-start(), calls=%async_computation.4 | async-start | bytes 262144 | tf_op jit(solution)/shard_map/psum | solution.py:32
  186.0 750.1 %all-gather.2.cloned.1.call-start = ((), (), s32[]{:S(2)}) async-start(), calls=%async_computation.5 | async-start | bytes 2162688 | tf_op jit(solution)/shard_map/all_gather | solution.py:47
  301.4 564.0 %copy-start = (f32[32,1024]{1,0:T(8,128)S(1)}, f32[32,1024]{1,0:T(8,128)}, u32[]{:S(2)}) copy-start(f32[32,1024]{1,0:T(8,128)} %all-reduce.3.cloned.1.call-done) | copy-start | bytes 393220
  402.4 46.0 %copy-start.2 = (f32[32]{0:T(128)}, f32[32]{0:T(128)S(1)}, u32[]{:S(2)}) copy-start(f32[32]{0:T(128)S(1)} %fusion.24) | copy-start | bytes 388 | tf_op jit(solution)/shard_map/while
  448.7 46.0 %copy-start.2 = (f32[32]{0:T(128)}, f32[32]{0:T(128)S(1)}, u32[]{:S(2)}) copy-start(f32[32]{0:T(128)S(1)} %fusion.24) | copy-start | bytes 388 | tf_op jit(solution)/shard_map/while
  494.9 46.0 %copy-start.2 = (f32[32]{0:T(128)}, f32[32]{0:T(128)S(1)}, u32[]{:S(2)}) copy-start(f32[32]{0:T(128)S(1)} %fusion.24) | copy-start | bytes 388 | tf_op jit(solution)/shard_map/while
  541.2 46.0 %copy-start.2 = (f32[32]{0:T(128)}, f32[32]{0:T(128)S(1)}, u32[]{:S(2)}) copy-start(f32[32]{0:T(128)S(1)} %fusion.24) | copy-start | bytes 388 | tf_op jit(solution)/shard_map/while
  587.4 46.0 %copy-start.2 = (f32[32]{0:T(128)}, f32[32]{0:T(128)S(1)}, u32[]{:S(2)}) copy-start(f32[32]{0:T(128)S(1)} %fusion.24) | copy-start | bytes 388 | tf_op jit(solution)/shard_map/while
  633.7 46.0 %copy-start.2 = (f32[32]{0:T(128)}, f32[32]{0:T(128)S(1)}, u32[]{:S(2)}) copy-start(f32[32]{0:T(128)S(1)} %fusion.24) | copy-start | bytes 388 | tf_op jit(solution)/shard_map/while
  680.0 46.0 %copy-start.2 = (f32[32]{0:T(128)}, f32[32]{0:T(128)S(1)}, u32[]{:S(2)}) copy-start(f32[32]{0:T(128)S(1)} %fusion.24) | copy-start | bytes 388 | tf_op jit(solution)/shard_map/while
  726.2 46.0 %copy-start.2 = (f32[32]{0:T(128)}, f32[32]{0:T(128)S(1)}, u32[]{:S(2)}) copy-start(f32[32]{0:T(128)S(1)} %fusion.24) | copy-start | bytes 388 | tf_op jit(solution)/shard_map/while
  772.5 46.0 %copy-start.2 = (f32[32]{0:T(128)}, f32[32]{0:T(128)S(1)}, u32[]{:S(2)}) copy-start(f32[32]{0:T(128)S(1)} %fusion.24) | copy-start | bytes 388 | tf_op jit(solution)/shard_map/while
  818.7 46.0 %copy-start.2 = (f32[32]{0:T(128)}, f32[32]{0:T(128)S(1)}, u32[]{:S(2)}) copy-start(f32[32]{0:T(128)S(1)} %fusion.24) | copy-start | bytes 388 | tf_op jit(solution)/shard_map/while
Sparse Core Ops, SparseCore 0:
  83.5 102.4 reduce-scatter.1
  189.2 112.2 all-reduce.2
  866.3 69.8 all-gather.1
where the time goes:
time: 1010 us
  blocking collectives  690 us (68%)
  waiting for transfers between devices  283 us (28%)
  between operations  14.4 us (1%)
  matrix products  10.1 us (1%)
    psum x10, blocking collectives, column_total(): return lax.psum(values, 'mem')  458 us
    psum x1, waiting for transfers between devices, per_device(): gram_rows = lax.psum(local_rows, 'space')  114 us
    reduce_scatter x1, waiting for transfers between devices, per_device(): lax.psum_scatter(partial_gram, 'mem', scatter_dimension=0, tiled=True)  98.8 us
    all_to_all x1, blocking collectives, per_device(): lax.all_to_all(ensemble, 'mem', split_axis=1, concat_axis=0, tiled=True)  72.3 us
    all_gather x1, waiting for transfers between devices, per_device(): coupling = lax.all_gather(coupling_rows, 'mem', axis=0, tiled=True)  70 us
    all_to_all x1, blocking collectives, per_device(): return lax.all_to_all(mixed, 'mem', split_axis=0, concat_axis=1, tiled=True)  63.8 us
    unnamed x1, blocking collectives  48.6 us
    psum x1, blocking collectives, per_device(): dist_total = lax.psum(jnp.sum(dist), 'mem')  47.1 us
  transfers between devices with their start and end apart: 3, of which 3 were waited for; matrix products, arithmetic and copies ran while one was open for 0% of the time, Pallas kernels for 0%

commit v1 on v0

--- a/solution.py
+++ b/solution.py
@@ -41,7 +41,7 @@
     weights_rows = lax.dynamic_slice_in_dim(weights, start, members_dev, 0)
 
     def column_total(values):
-        return lax.psum(values, "mem")
+        return jnp.sum(lax.all_gather(values, "mem"), axis=0)
 
     coupling_rows = coupling_from(kernel, weights_rows, column_total)
     coupling = lax.all_gather(coupling_rows, "mem", axis=0, tiled=True)

time: 1010 us -> 835 us (0.83)
  blocking collectives: 690 us -> 516 us
    psum x10 -> x0, blocking collectives: 458 us -> none  [column_total(): return lax.psum(values, 'mem')]
    all_gather x0 -> x10, blocking collectives: none -> 284 us  [column_total(): return jnp.sum(lax.all_gather(values, 'mem'), axis=0)]
  transfers between devices with their start and end apart: 3 -> 3, of which waited for: 3 -> 3; matrix products, arithmetic and copies ran while one was open for 0% -> 1% of each run, Pallas kernels for 0% -> 0%
where the time goes in v1:
time: 835 us; the launch traced here: 834 us
  blocking collectives  516 us (62%)
  waiting for transfers between devices  280 us (34%)
  between operations  14.4 us (2%)
  matrix products  10.1 us (1%)
    all_gather x10, blocking collectives, column_total(): return jnp.sum(lax.all_gather(values, 'mem'), axis=0)  284 us
    psum x1, waiting for transfers between devices, per_device(): gram_rows = lax.psum(local_rows, 'space')  114 us
    reduce_scatter x1, waiting for transfers between devices, per_device(): lax.psum_scatter(partial_gram, 'mem', scatter_dimension=0, tiled=True)  98.8 us
    all_to_all x1, blocking collectives, per_device(): lax.all_to_all(ensemble, 'mem', split_axis=1, concat_axis=0, tiled=True)  72.3 us
    all_gather x1, waiting for transfers between devices, per_device(): coupling = lax.all_gather(coupling_rows, 'mem', axis=0, tiled=True)  67.1 us
    all_to_all x1, blocking collectives, per_device(): return lax.all_to_all(mixed, 'mem', split_axis=0, concat_axis=1, tiled=True)  63.8 us
    unnamed x1, blocking collectives  48.6 us
    psum x1, blocking collectives, per_device(): dist_total = lax.psum(jnp.sum(dist), 'mem')  47.1 us
  transfers between devices with their start and end apart: 3, of which 3 were waited for; matrix products, arithmetic and copies ran while one was open for 1% of the time, Pallas kernels for 0%

profile of v1, /device:TPU:1, one launch (start us, length us, event | category | flops | bytes accessed | tf_op | source)
XLA Modules:
  0.0 834.1 jit_solution(5743135458448848651)
XLA Ops:
  6.5 1.4 copy.14
  7.9 72.3 %all_to_all.38 = bf16[32,32,512]{2,0,1:T(8,128)(2,1)S(1)} all-to-all(bf16[32,32,512]{2,0,1:T(8,128)(2,1)S(1)} %bitcast.43), channel_id=1, replica_groups=mesh['mem'=32,'space'=16] {'mem'}, dimensions={1} | all-to-all | bytes 2097152 | tf_op jit(solution)/shard_map/all_to_all | solution.py:26
  80.2 3.2 fusion.6
  83.5 1.3 dynamic-slice
  85.3 0.6 reduce_max.9
  85.9 1.2 fusion.5
  87.2 98.8 %reduce-scatter.2.cloned.1.call-done = f32[32,1024]{1,0:T(8,128)} async-done(((f32[1024,1024]{1,0:T(8,128)}), f32[32,1024]{1,0:T(8,128)}) %reduce-scatter.2.cloned.1.call-update) | async-done | bytes 131088 | tf_op jit(solution)/shard_map/reduce_scatter | solution.py:31
  186.1 1.2 fusion.4
  187.4 114.0 %all-reduce.3.cloned.1.call-done = f32[32,1024]{1,0:T(8,128)} async-done(((f32[32,1024]{1,0:T(8,128)}), f32[32,1024]{1,0:T(8,128)}) %all-reduce.3.cloned.1.call-update) | async-done | bytes 131088 | tf_op jit(solution)/shard_map/psum | solution.py:32
  301.4 0.9 select_reduce_fusion
  302.6 48.6 %all-reduce = f32[1024]{0:T(1024)S(1)} all-reduce(f32[1024]{0:T(1024)S(1)} %dynamic-update-slice), channel_id=1, replica_groups=mesh['mem'=32,'space'=16] {'mem'}, use_global_device_ids=true, to_apply=%add | all-reduce | flops 1024 | bytes 8192
  351.2 1.7 fusion.3
  352.8 0.5 copy.18
  353.3 47.1 %psum.15 = f32[]{:T(128)} all-reduce(f32[]{:T(128)} %fusion.3), channel_id=1, replica_groups=mesh['mem'=32,'space'=16] {'mem'}, use_global_device_ids=true, to_apply=%region_6.0 | all-reduce | flops 1 | bytes 8 | tf_op jit(solution)/shard_map/psum | solution.py:38
  401.1 1.0 divide_exponential_fusion
  402.1 289.4 %while.13 = (s32[]{:T(128)}, f32[32]{0:T(128)}, f32[1024]{0:T(1024)S(1)}, f32[32,1024]{1,0:T(8,128)S(1)}, f32[32]{0:T(128)S(1)}, /*index=5*/s32[]{:T(128)}, s32[]{:T(128)}, f32[]{:T(128)}) while((s32[]{:T(128)}, f32[32]{0:T(128)}, f32[1024]{0:T(1024)S(1)}, f32[32,1024]{1,0:T(8,128)S(1)}, f32[32]{0:T(128)S(1)}, ...), condition=%wide.region_9.0_spmd.clone, body=%wide.region_7.0_spmd.clone.sunk | while | flops 820259 | bytes 820223 | solution.py:19
  402.6 27.9 %all-gather.3 = f32[32768]{0:T(1024)S(1)} all-gather(f32[1024]{0:T(1024)S(1)} %bitcast.48), channel_id=2, replica_groups=mesh['mem'=32,'space'=16] {'mem'}, dimensions={0}, use_global_device_ids=true | all-gather | bytes 135168 | tf_op jit(solution)/shard_map/while/body/eval_jaxpr/all_gather | solution.py:44
  431.0 30.3 %all-gather.3 = f32[32768]{0:T(1024)S(1)} all-gather(f32[1024]{0:T(1024)S(1)} %bitcast.48), channel_id=2, replica_groups=mesh['mem'=32,'space'=16] {'mem'}, dimensions={0}, use_global_device_ids=true | all-gather | bytes 135168 | tf_op jit(solution)/shard_map/while/body/eval_jaxpr/all_gather | solution.py:44
  461.8 27.5 %all-gather.3 = f32[32768]{0:T(1024)S(1)} all-gather(f32[1024]{0:T(1024)S(1)} %bitcast.48), channel_id=2, replica_groups=mesh['mem'=32,'space'=16] {'mem'}, dimensions={0}, use_global_device_ids=true | all-gather | bytes 135168 | tf_op jit(solution)/shard_map/while/body/eval_jaxpr/all_gather | solution.py:44
  489.8 29.8 %all-gather.3 = f32[32768]{0:T(1024)S(1)} all-gather(f32[1024]{0:T(1024)S(1)} %bitcast.48), channel_id=2, replica_groups=mesh['mem'=32,'space'=16] {'mem'}, dimensions={0}, use_global_device_ids=true | all-gather | bytes 135168 | tf_op jit(solution)/shard_map/while/body/eval_jaxpr/all_gather | solution.py:44
  520.0 27.5 %all-gather.3 = f32[32768]{0:T(1024)S(1)} all-gather(f32[1024]{0:T(1024)S(1)} %bitcast.48), channel_id=2, replica_groups=mesh['mem'=32,'space'=16] {'mem'}, dimensions={0}, use_global_device_ids=true | all-gather | bytes 135168 | tf_op jit(solution)/shard_map/while/body/eval_jaxpr/all_gather | solution.py:44
  548.0 28.8 %all-gather.3 = f32[32768]{0:T(1024)S(1)} all-gather(f32[1024]{0:T(1024)S(1)} %bitcast.48), channel_id=2, replica_groups=mesh['mem'=32,'space'=16] {'mem'}, dimensions={0}, use_global_device_ids=true | all-gather | bytes 135168 | tf_op jit(solution)/shard_map/while/body/eval_jaxpr/all_gather | solution.py:44
  577.3 27.5 %all-gather.3 = f32[32768]{0:T(1024)S(1)} all-gather(f32[1024]{0:T(1024)S(1)} %bitcast.48), channel_id=2, replica_groups=mesh['mem'=32,'space'=16] {'mem'}, dimensions={0}, use_global_device_ids=true | all-gather | bytes 135168 | tf_op jit(solution)/shard_map/while/body/eval_jaxpr/all_gather | solution.py:44
  605.3 28.8 %all-gather.3 = f32[32768]{0:T(1024)S(1)} all-gather(f32[1024]{0:T(1024)S(1)} %bitcast.48), channel_id=2, replica_groups=mesh['mem'=32,'space'=16] {'mem'}, dimensions={0}, use_global_device_ids=true | all-gather | bytes 135168 | tf_op jit(solution)/shard_map/while/body/eval_jaxpr/all_gather | solution.py:44
  634.6 27.5 %all-gather.3 = f32[32768]{0:T(1024)S(1)} all-gather(f32[1024]{0:T(1024)S(1)} %bitcast.48), channel_id=2, replica_groups=mesh['mem'=32,'space'=16] {'mem'}, dimensions={0}, use_global_device_ids=true | all-gather | bytes 135168 | tf_op jit(solution)/shard_map/while/body/eval_jaxpr/all_gather | solution.py:44
  662.6 28.8 %all-gather.3 = f32[32768]{0:T(1024)S(1)} all-gather(f32[1024]{0:T(1024)S(1)} %bitcast.48), channel_id=2, replica_groups=mesh['mem'=32,'space'=16] {'mem'}, dimensions={0}, use_global_device_ids=true | all-gather | bytes 135168 | tf_op jit(solution)/shard_map/while/body/eval_jaxpr/all_gather | solution.py:44
  691.5 0.6 broadcast_multiply_fusion
  692.1 0.7 multiply_convert_fusion
  692.9 67.1 %all-gather.6.cloned.1.call-done = bf16[1024,1024]{1,0:T(8,128)(2,1)} async-done(((bf16[32,1024]{1,0:T(8,128)(2,1)}), bf16[1024,1024]{1,0:T(8,128)(2,1)}) %all-gather.6.cloned.1.call-update) | async-done | bytes 2097168 | tf_op jit(solution)/shard_map/all_gather | solution.py:47
  759.9 2.9 convolution_convert_fusion
  762.8 63.8 %all_to_all.39 = bf16[32,32,512]{2,1,0:T(8,128)(2,1)S(1)} all-to-all(bf16[32,32,512]{2,1,0:T(8,128)(2,1)S(1)} %bitcast.47), channel_id=1, replica_groups=mesh['mem'=32,'space'=16] {'mem'}, dimensions={0} | all-to-all | bytes 2097152 | tf_op jit(solution)/shard_map/all_to_all | solution.py:52
  826.5 1.1 copy.12
  (94 shorter events, 5.1 us)
Async XLA Ops:
  6.5 179.5 %reduce-scatter.2.cloned.1.call-start = ((), (), s32[]{:S(2)}) async-start(), calls=%async_computation.3 | async-start | bytes 4325376 | tf_op jit(solution)/shard_map/reduce_scatter | solution.py:31
  83.4 1.9 copy-start.1
  83.4 218.0 %all-reduce.3.cloned.1.call-start = ((), (), s32[]{:S(2)}) async-start(), calls=%async_computation.4 | async-start | bytes 262144 | tf_op jit(solution)/shard_map/psum | solution.py:32
  186.0 573.9 %all-gather.6.cloned.1.call-start = ((), (), s32[]{:S(2)}) async-start(), calls=%async_computation.5 | async-start | bytes 2162688 | tf_op jit(solution)/shard_map/all_gather | solution.py:47
  402.1 290.0 %copy-start = (f32[32,1024]{1,0:T(8,128)S(1)}, f32[32,1024]{1,0:T(8,128)}, u32[]{:S(2)}) copy-start(f32[32,1024]{1,0:T(8,128)} %all-reduce.3.cloned.1.call-done) | copy-start | bytes 393220
  402.3 28.2 %copy-start.2 = (f32[32]{0:T(128)}, f32[32]{0:T(128)S(1)}, u32[]{:S(2)}) copy-start(f32[32]{0:T(128)S(1)} %fusion.24) | copy-start | bytes 388 | tf_op jit(solution)/shard_map/while
  430.7 30.6 %copy-start.2 = (f32[32]{0:T(128)}, f32[32]{0:T(128)S(1)}, u32[]{:S(2)}) copy-start(f32[32]{0:T(128)S(1)} %fusion.24) | copy-start | bytes 388 | tf_op jit(solution)/shard_map/while
  461.5 27.8 %copy-start.2 = (f32[32]{0:T(128)}, f32[32]{0:T(128)S(1)}, u32[]{:S(2)}) copy-start(f32[32]{0:T(128)S(1)} %fusion.24) | copy-start | bytes 388 | tf_op jit(solution)/shard_map/while
  489.5 30.1 %copy-start.2 = (f32[32]{0:T(128)}, f32[32]{0:T(128)S(1)}, u32[]{:S(2)}) copy-start(f32[32]{0:T(128)S(1)} %fusion.24) | copy-start | bytes 388 | tf_op jit(solution)/shard_map/while
  519.8 27.8 %copy-start.2 = (f32[32]{0:T(128)}, f32[32]{0:T(128)S(1)}, u32[]{:S(2)}) copy-start(f32[32]{0:T(128)S(1)} %fusion.24) | copy-start | bytes 388 | tf_op jit(solution)/shard_map/while
  547.8 29.1 %copy-start.2 = (f32[32]{0:T(128)}, f32[32]{0:T(128)S(1)}, u32[]{:S(2)}) copy-start(f32[32]{0:T(128)S(1)} %fusion.24) | copy-start | bytes 388 | tf_op jit(solution)/shard_map/while
  577.1 27.8 %copy-start.2 = (f32[32]{0:T(128)}, f32[32]{0:T(128)S(1)}, u32[]{:S(2)}) copy-start(f32[32]{0:T(128)S(1)} %fusion.24) | copy-start | bytes 388 | tf_op jit(solution)/shard_map/while
  605.1 29.1 %copy-start.2 = (f32[32]{0:T(128)}, f32[32]{0:T(128)S(1)}, u32[]{:S(2)}) copy-start(f32[32]{0:T(128)S(1)} %fusion.24) | copy-start | bytes 388 | tf_op jit(solution)/shard_map/while
  634.4 27.8 %copy-start.2 = (f32[32]{0:T(128)}, f32[32]{0:T(128)S(1)}, u32[]{:S(2)}) copy-start(f32[32]{0:T(128)S(1)} %fusion.24) | copy-start | bytes 388 | tf_op jit(solution)/shard_map/while
  662.4 29.1 %copy-start.2 = (f32[32]{0:T(128)}, f32[32]{0:T(128)S(1)}, u32[]{:S(2)}) copy-start(f32[32]{0:T(128)S(1)} %fusion.24) | copy-start | bytes 388 | tf_op jit(solution)/shard_map/while
Sparse Core Ops, SparseCore 0:
  83.5 102.4 reduce-scatter.1
  189.2 112.2 all-reduce.2
  693.0 66.8 all-gather.5
